TPU v7x, 256 devices: a whole 4x4x8 slice. The times are simulated.
256 devices in a mesh: section: 4 (over z_lo), rep: 8 (over y, core), tp: 8 (over z_hi, x).
Axes of the slice: x: 4, y: 4, z: 8 (z_hi: 2, z_lo: 4; z = z_hi * 4 + z_lo), core: 2. Of those that a mesh axis runs over, the one named last changes fastest.
Arguments:
- acts: bfloat16 [8, 256, 896], P('rep', None, 'tp'), may hold values from -6 to 6
- cotangent: bfloat16 [8, 256, 896], P('rep', None, 'tp'), may hold values from -8.5 to 8.5
- w_gate: bfloat16 [4, 8, 896, 4864], P('section', 'rep', None, 'tp'), may hold values from -3 to 3
- w_up: bfloat16 [4, 8, 896, 4864], P('section', 'rep', None, 'tp'), may hold values from -3 to 3
- w_down: bfloat16 [4, 8, 4864, 896], P('section', 'rep', 'tp'), may hold values from -4.2 to 4.2
- m_gate: bfloat16 [4, 8, 896, 4864], P('section', 'rep', None, 'tp'), may hold values from -0.099609375 to 0.099609375
- m_up: bfloat16 [4, 8, 896, 4864], P('section', 'rep', None, 'tp'), may hold values from -0.099609375 to 0.099609375
- m_down: bfloat16 [4, 8, 4864, 896], P('section', 'rep', 'tp'), may hold values from -0.099609375 to 0.099609375
- v_gate: bfloat16 [4, 8, 896, 4864], P('section', 'rep', None, 'tp'), may hold values from 0.0009994507 to 0.099609375
- v_up: bfloat16 [4, 8, 896, 4864], P('section', 'rep', None, 'tp'), may hold values from 0.0009994507 to 0.099609375
- v_down: bfloat16 [4, 8, 4864, 896], P('section', 'rep', 'tp'), may hold values from 0.0009994507 to 0.099609375
- steps: int32 [4], P('section'), may hold values from 0 to 999
Outputs:
- section_out: bfloat16 [4, 8, 256, 896], P('section', 'rep', None, 'tp')
- section_in_grad: bfloat16 [4, 8, 256, 896], P('section', 'rep', None, 'tp')
- new_gate: bfloat16 [4, 8, 896, 4864], P('section', 'rep', None, 'tp')
- new_up: bfloat16 [4, 8, 896, 4864], P('section', 'rep', None, 'tp')
- new_down: bfloat16 [4, 8, 4864, 896], P('section', 'rep', 'tp')
All inputs are finite; a program needn't handle non-finite values.
Results may differ from a plain program's by a relative error of at most 0.023.
Values may be sent and summed in bfloat16 or wider, within the bound.
A program may use at most 128 MiB of HBM per device.

v0:
```python
import functools
import math
import jax
import jax.numpy as jnp
from jax import lax
from jax.sharding import PartitionSpec as P

D = 896
FF = 4864
TOK = 128
MB = 2
NORM_EPS = 1e-06
ADAM_EPS = 1e-08
LEARN = 0.3
BETA_ONE = 0.9
BETA_TWO = 0.95


def as_sent(array):
    return jax.tree.map(lambda a: a.astype(jnp.bfloat16) if a.dtype == jnp.float32 else a, array)


def from_behind(array, axis, by):
    peers = lax.axis_size(axis)
    return lax.ppermute(array, axis, [(i, (i + by) % peers) for i in range(peers)])


def passed_along(value, axis, steps):
    count = lax.axis_size(axis)
    first, last = (max(0, -steps), min(count, count - steps))
    return lax.ppermute(value, axis, [(source, source + steps) for source in range(first, last)])


def widen(value):
    return lax.all_gather(value, "tp", axis=1, tiled=True)


def norm_parts(x_full):
    xf = x_full.astype(jnp.float32)
    rms = jnp.sqrt(jnp.mean(xf * xf, axis=1, keepdims=True) + NORM_EPS)
    normed = xf / rms
    normed_b = normed.astype(jnp.bfloat16)
    return (xf, rms, normed, normed_b)


def forward_parts(x_full, wg, wu):
    xf, rms, normed, normed_b = norm_parts(x_full)
    gate = jnp.dot(normed_b, wg, preferred_element_type=jnp.float32) * (1.0 / math.sqrt(D))
    upper = jnp.dot(normed_b, wu, preferred_element_type=jnp.float32) * (1.0 / math.sqrt(D))
    return (xf, rms, normed, normed_b, gate, upper)


def adam_step(weight, first, second, grad):
    m_new = BETA_ONE * first.astype(jnp.float32) + (1.0 - BETA_ONE) * grad
    v_new = BETA_TWO * second.astype(jnp.float32) + (1.0 - BETA_TWO) * grad * grad
    return (weight.astype(jnp.float32) - LEARN * m_new / (jnp.sqrt(v_new) + ADAM_EPS)).astype(
        jnp.bfloat16
    )


def partner_mean(stacked, distance):
    other = jax.tree.map(
        lambda part, own: part.astype(own.dtype),
        from_behind(as_sent(stacked), "rep", distance),
        stacked,
    )
    return ((stacked.astype(jnp.float32) + other.astype(jnp.float32)) * 0.5).astype(jnp.bfloat16)


def contract(left, right, left_dim, right_dim):
    return lax.dot_general(
        left, right, (((left_dim,), (right_dim,)), ((), ())), preferred_element_type=jnp.float32
    )


def on_device(
    acts, cotangent, w_gate, w_up, w_down, m_gate, m_up, m_down, v_gate, v_up, v_down, steps
):
    section = lax.axis_index("section")
    sections = lax.axis_size("section")
    part = lax.axis_index("tp")
    local_width = acts.shape[2]
    wg = w_gate[0, 0]
    wu = w_up[0, 0]
    wd = w_down[0, 0]
    local_hidden = wg.shape[1]
    inv_ff = 1.0 / math.sqrt(FF)
    ticks = MB + sections - 1
    inputs = acts[0].reshape(MB, TOK, local_width)
    cots = cotangent[0].reshape(MB, TOK, local_width)
    saved = jnp.zeros((MB, TOK, D), jnp.bfloat16)
    gate_saved = jnp.zeros((MB, TOK, local_hidden), jnp.float32)
    upper_saved = jnp.zeros((MB, TOK, local_hidden), jnp.float32)
    out_buf = jnp.zeros((MB, TOK, local_width), jnp.bfloat16)
    incoming = jnp.zeros((TOK, local_width), jnp.bfloat16)
    for tick in range(ticks):
        micro = tick - section
        valid = (micro >= 0) & (micro < MB)
        place = jnp.clip(micro, 0, MB - 1)
        first = lax.dynamic_index_in_dim(inputs, place, 0, keepdims=False)
        x_local = jnp.where(section == 0, first, incoming)
        x_full = widen(x_local)
        xf, rms, normed, normed_b, gate, upper = forward_parts(x_full, wg, wu)
        hidden = (jax.nn.silu(gate) * upper).astype(jnp.bfloat16)
        partial_out = jnp.dot(hidden, wd, preferred_element_type=jnp.float32) * inv_ff
        share = lax.psum_scatter(
            partial_out.astype(jnp.bfloat16), "tp", scatter_dimension=1, tiled=True
        ).astype(jnp.float32)
        y_local = (x_local.astype(jnp.float32) + share).astype(jnp.bfloat16)
        if tick < ticks - 1:
            incoming = passed_along(y_local, "section", 1)
        saved = jnp.where(valid, lax.dynamic_update_index_in_dim(saved, x_full, place, 0), saved)
        gate_saved = jnp.where(
            valid, lax.dynamic_update_index_in_dim(gate_saved, gate, place, 0), gate_saved
        )
        upper_saved = jnp.where(
            valid, lax.dynamic_update_index_in_dim(upper_saved, upper, place, 0), upper_saved
        )
        out_buf = jnp.where(
            valid, lax.dynamic_update_index_in_dim(out_buf, y_local, place, 0), out_buf
        )
    acc_gate = jnp.zeros(wg.shape, jnp.float32)
    acc_up = jnp.zeros(wu.shape, jnp.float32)
    acc_down = jnp.zeros(wd.shape, jnp.float32)
    grad_buf = jnp.zeros((MB, TOK, local_width), jnp.bfloat16)
    incoming_back = jnp.zeros((TOK, local_width), jnp.bfloat16)
    for tick in range(ticks):
        micro = tick - (sections - 1 - section)
        valid = (micro >= 0) & (micro < MB)
        place = jnp.clip(micro, 0, MB - 1)
        last_cot = lax.dynamic_index_in_dim(cots, place, 0, keepdims=False)
        dy_local = jnp.where(section == sections - 1, last_cot, incoming_back)
        dy_full = widen(dy_local)
        x_full = lax.dynamic_index_in_dim(saved, place, 0, keepdims=False)
        xf, rms, normed, normed_b = norm_parts(x_full)
        gate = lax.dynamic_index_in_dim(gate_saved, place, 0, keepdims=False)
        upper = lax.dynamic_index_in_dim(upper_saved, place, 0, keepdims=False)
        sig = jax.nn.sigmoid(gate)
        active = gate * sig
        hidden = (active * upper).astype(jnp.bfloat16)
        dh = contract(dy_full, wd, 1, 1) * inv_ff
        dgate = (dh * upper * sig * (1.0 + gate * (1.0 - sig))).astype(jnp.bfloat16)
        dup = (dh * active).astype(jnp.bfloat16)
        acc_down = acc_down + jnp.where(valid, contract(hidden, dy_full, 0, 0) * inv_ff, 0.0)
        acc_gate = acc_gate + jnp.where(
            valid, contract(normed_b, dgate, 0, 0) * (1.0 / math.sqrt(D)), 0.0
        )
        acc_up = acc_up + jnp.where(
            valid, contract(normed_b, dup, 0, 0) * (1.0 / math.sqrt(D)), 0.0
        )
        partial_in = (contract(dgate, wg, 1, 1) + contract(dup, wu, 1, 1)) * (1.0 / math.sqrt(D))
        dnorm_local = lax.psum_scatter(
            partial_in.astype(jnp.bfloat16), "tp", scatter_dimension=1, tiled=True
        ).astype(jnp.float32)
        normed_local = lax.dynamic_slice_in_dim(normed, part * local_width, local_width, 1)
        stat = lax.psum(jnp.sum(dnorm_local * normed_local, axis=1), "tp") / D
        dx_local = (
            dy_local.astype(jnp.float32) + (dnorm_local - normed_local * stat[:, None]) / rms
        ).astype(jnp.bfloat16)
        grad_buf = jnp.where(
            valid, lax.dynamic_update_index_in_dim(grad_buf, dx_local, place, 0), grad_buf
        )
        if tick < ticks - 1:
            incoming_back = passed_along(dx_local, "section", -1)
    new_gate_local = adam_step(wg, m_gate[0, 0], v_gate[0, 0], acc_gate)
    new_up_local = adam_step(wu, m_up[0, 0], v_up[0, 0], acc_up)
    new_down_local = adam_step(wd, m_down[0, 0], v_down[0, 0], acc_down)
    flat_size = wg.shape[0] * wg.shape[1]
    stacked = jnp.stack(
        [
            new_gate_local.reshape(flat_size),
            new_up_local.reshape(flat_size),
            new_down_local.reshape(flat_size),
        ]
    )
    levels = lax.axis_size("rep").bit_length() - 1
    branches = [functools.partial(partner_mean, distance=2**level) for level in range(levels)]
    which = steps[0] % levels
    averaged = lax.switch(which, branches, stacked)
    new_gate = averaged[0].reshape(wg.shape)[None, None]
    new_up = averaged[1].reshape(wu.shape)[None, None]
    new_down = averaged[2].reshape(wd.shape)[None, None]
    section_out = out_buf.reshape(1, 1, MB * TOK, local_width)
    section_in_grad = grad_buf.reshape(1, 1, MB * TOK, local_width)
    return (section_out, section_in_grad, new_gate, new_up, new_down)


def solution(mesh):
    return jax.shard_map(
        on_device,
        mesh=mesh,
        in_specs=(
            P("rep", None, "tp"),
            P("rep", None, "tp"),
            P("section", "rep", None, "tp"),
            P("section", "rep", None, "tp"),
            P("section", "rep", "tp", None),
            P("section", "rep", None, "tp"),
            P("section", "rep", None, "tp"),
            P("section", "rep", "tp", None),
            P("section", "rep", None, "tp"),
            P("section", "rep", None, "tp"),
            P("section", "rep", "tp", None),
            P("section"),
        ),
        out_specs=(
            P("section", "rep", None, "tp"),
            P("section", "rep", None, "tp"),
            P("section", "rep", None, "tp"),
            P("section", "rep", None, "tp"),
            P("section", "rep", "tp", None),
        ),
        check_vma=False,
    )
```

profile of v0, /device:TPU:66, one launch (start us, length us, event | category | flops | bytes accessed | tf_op | source)
XLA Modules:
  0.0 1532.5 jit_solution(6093599195167706535)
XLA Ops:
  9.0 44.1 %all-gather = bf16[1,128,896]{1,2,0:T(8,128)(2,1)S(1)} all-gather(bf16[1,128,112]{1,2,0:T(8,128)(2,1)S(1)} %copy_select_fusion.1), channel_id=2, replica_groups=mesh['section'=4,'rep'=8,'tp'=8] {'tp'}, dimensions={2}, use_global_device_ids=true | all-gather | bytes 258048 | tf_op jit(solution)/shard_map/all_gather | solution.py:35
  59.2 76.5 %reduce-scatter.11.cloned.1.call-done = bf16[128,112]{0,1:T(8,128)(2,1)} async-done(((bf16[128,896]{0,1:T(8,128)(2,1)}), bf16[128,112]{0,1:T(8,128)(2,1)}) %reduce-scatter.11.cloned.1.call-update) | async-done | bytes 28688 | tf_op jit(solution)/shard_map/reduce_scatter | solution.py:106
  139.1 3.1 collective-permute-done.3
  142.3 40.6 %all_gather.31 = bf16[128,896]{0,1:T(8,128)(2,1)S(1)} all-gather(bf16[128,112]{0,1:T(8,128)(2,1)S(1)} %bitcast_select_fusion.19), channel_id=1, replica_groups=mesh['section'=4,'rep'=8,'tp'=8] {'tp'}, dimensions={1}, use_global_device_ids=true | all-gather | bytes 258048 | tf_op jit(solution)/shard_map/all_gather | solution.py:35
  187.2 76.0 %reduce-scatter.13.cloned.1.call-done = bf16[128,112]{0,1:T(8,128)(2,1)} async-done(((bf16[128,896]{0,1:T(8,128)(2,1)}), bf16[128,112]{0,1:T(8,128)(2,1)}) %reduce-scatter.13.cloned.1.call-update) | async-done | bytes 28688 | tf_op jit(solution)/shard_map/reduce_scatter | solution.py:106
  269.8 40.6 %all_gather.32 = bf16[128,896]{0,1:T(8,128)(2,1)S(1)} all-gather(bf16[128,112]{0,1:T(8,128)(2,1)S(1)} %bitcast_select_fusion.18), channel_id=1, replica_groups=mesh['section'=4,'rep'=8,'tp'=8] {'tp'}, dimensions={1}, use_global_device_ids=true | all-gather | bytes 258048 | tf_op jit(solution)/shard_map/all_gather | solution.py:35
  315.4 75.3 %reduce-scatter.15.cloned.1.call-done = bf16[128,112]{0,1:T(8,128)(2,1)} async-done(((bf16[128,896]{0,1:T(8,128)(2,1)}), bf16[128,112]{0,1:T(8,128)(2,1)}) %reduce-scatter.15.cloned.1.call-update) | async-done | bytes 28688 | tf_op jit(solution)/shard_map/reduce_scatter | solution.py:106
  394.1 43.8 %all-gather.1 = bf16[1,128,896]{1,2,0:T(8,128)(2,1)} all-gather(bf16[1,128,112]{1,2,0:T(8,128)(2,1)} %copy_select_fusion), channel_id=3, replica_groups=mesh['section'=4,'rep'=8,'tp'=8] {'tp'}, dimensions={2}, use_global_device_ids=true | all-gather | bytes 258048 | tf_op jit(solution)/shard_map/all_gather | solution.py:35
  439.4 44.0 %all_gather.33 = bf16[128,896]{0,1:T(8,128)(2,1)S(1)} all-gather(bf16[128,112]{0,1:T(8,128)(2,1)S(1)} %bitcast_select_fusion.17), channel_id=1, replica_groups=mesh['section'=4,'rep'=8,'tp'=8] {'tp'}, dimensions={1}, use_global_device_ids=true | all-gather | bytes 258048 | tf_op jit(solution)/shard_map/all_gather | solution.py:35
  488.8 74.4 %reduce-scatter.17.cloned.1.call-done = bf16[128,112]{0,1:T(8,128)(2,1)} async-done(((bf16[128,896]{0,1:T(8,128)(2,1)}), bf16[128,112]{0,1:T(8,128)(2,1)}) %reduce-scatter.17.cloned.1.call-update) | async-done | bytes 28688 | tf_op jit(solution)/shard_map/reduce_scatter | solution.py:106
  570.6 41.1 %all_gather.34 = bf16[128,896]{0,1:T(8,128)(2,1)S(1)} all-gather(bf16[128,112]{0,1:T(8,128)(2,1)S(1)} %bitcast_select_fusion.16), channel_id=1, replica_groups=mesh['section'=4,'rep'=8,'tp'=8] {'tp'}, dimensions={1}, use_global_device_ids=true | all-gather | bytes 258048 | tf_op jit(solution)/shard_map/all_gather | solution.py:35
  626.2 2.8 fusion.139
  630.5 69.0 %reduce-scatter.21.cloned.1.call-done = bf16[128,112]{0,1:T(8,128)(2,1)} async-done(((bf16[128,896]{0,1:T(8,128)(2,1)}), bf16[128,112]{0,1:T(8,128)(2,1)}) %reduce-scatter.21.cloned.1.call-update) | async-done | bytes 28688 | tf_op jit(solution)/shard_map/reduce_scatter | solution.py:152
  700.4 24.6 %psum.35 = f32[128]{0:T(128)S(1)} all-reduce(f32[128]{0:T(128)S(1)} %fusion.173), channel_id=1, replica_groups=mesh['section'=4,'rep'=8,'tp'=8] {'tp'}, use_global_device_ids=true, to_apply=%region_13.14 | all-reduce | flops 128 | bytes 1024 | tf_op jit(solution)/shard_map/psum | solution.py:156
  725.9 3.2 collective-permute-start.7
  729.2 47.1 %reduce-scatter.19.cloned.1.call-done = bf16[128,112]{0,1:T(8,128)(2,1)} async-done(((bf16[128,896]{0,1:T(8,128)(2,1)}), bf16[128,112]{0,1:T(8,128)(2,1)}) %reduce-scatter.19.cloned.1.call-update) | async-done | bytes 28688 | tf_op jit(solution)/shard_map/reduce_scatter | solution.py:106
  779.1 40.6 %all_gather.36 = bf16[128,896]{0,1:T(8,128)(2,1)S(1)} all-gather(bf16[128,112]{0,1:T(8,128)(2,1)S(1)} %bitcast_select_fusion.15), channel_id=1, replica_groups=mesh['section'=4,'rep'=8,'tp'=8] {'tp'}, dimensions={1}, use_global_device_ids=true | all-gather | bytes 258048 | tf_op jit(solution)/shard_map/all_gather | solution.py:35
  824.0 2.8 fusion.165
  826.8 2.9 fusion.143
  829.7 70.5 %reduce-scatter.23.cloned.1.call-done = bf16[128,112]{0,1:T(8,128)(2,1)} async-done(((bf16[128,896]{0,1:T(8,128)(2,1)}), bf16[128,112]{0,1:T(8,128)(2,1)}) %reduce-scatter.23.cloned.1.call-update) | async-done | bytes 28688 | tf_op jit(solution)/shard_map/reduce_scatter | solution.py:152
  901.0 24.6 %psum.36 = f32[128]{0:T(128)S(1)} all-reduce(f32[128]{0:T(128)S(1)} %fusion.177), channel_id=1, replica_groups=mesh['section'=4,'rep'=8,'tp'=8] {'tp'}, use_global_device_ids=true, to_apply=%region_17.18 | all-reduce | flops 128 | bytes 1024 | tf_op jit(solution)/shard_map/psum | solution.py:156
  926.6 3.3 collective-permute-start.8
  929.9 2.8 fusion.167
  933.3 39.7 %all_gather.37 = bf16[128,896]{0,1:T(8,128)(2,1)S(1)} all-gather(bf16[128,112]{0,1:T(8,128)(2,1)S(1)} %bitcast_select_fusion.14), channel_id=1, replica_groups=mesh['section'=4,'rep'=8,'tp'=8] {'tp'}, dimensions={1}, use_global_device_ids=true | all-gather | bytes 258048 | tf_op jit(solution)/shard_map/all_gather | solution.py:35
  979.8 2.8 fusion.145
  982.6 75.5 %reduce-scatter.25.cloned.1.call-done = bf16[128,112]{0,1:T(8,128)(2,1)} async-done(((bf16[128,896]{0,1:T(8,128)(2,1)}), bf16[128,112]{0,1:T(8,128)(2,1)}) %reduce-scatter.25.cloned.1.call-update) | async-done | bytes 28688 | tf_op jit(solution)/shard_map/reduce_scatter | solution.py:152
  1059.0 24.6 %psum.37 = f32[128]{0:T(128)S(1)} all-reduce(f32[128]{0:T(128)S(1)} %fusion.181), channel_id=1, replica_groups=mesh['section'=4,'rep'=8,'tp'=8] {'tp'}, use_global_device_ids=true, to_apply=%region_21.22 | all-reduce | flops 128 | bytes 1024 | tf_op jit(solution)/shard_map/psum | solution.py:156
  1084.5 3.3 collective-permute-start.9
  1091.2 40.0 %all_gather.38 = bf16[128,896]{0,1:T(8,128)(2,1)S(1)} all-gather(bf16[128,112]{0,1:T(8,128)(2,1)S(1)} %bitcast_select_fusion.13), channel_id=1, replica_groups=mesh['section'=4,'rep'=8,'tp'=8] {'tp'}, dimensions={1}, use_global_device_ids=true | all-gather | bytes 258048 | tf_op jit(solution)/shard_map/all_gather | solution.py:35
  1138.0 2.9 fusion.147
  1140.9 75.4 %reduce-scatter.27.cloned.1.call-done = bf16[128,112]{0,1:T(8,128)(2,1)} async-done(((bf16[128,896]{0,1:T(8,128)(2,1)}), bf16[128,112]{0,1:T(8,128)(2,1)}) %reduce-scatter.27.cloned.1.call-update) | async-done | bytes 28688 | tf_op jit(solution)/shard_map/reduce_scatter | solution.py:152
  1217.2 24.6 %psum.38 = f32[128]{0:T(128)S(1)} all-reduce(f32[128]{0:T(128)S(1)} %fusion.185), channel_id=1, replica_groups=mesh['section'=4,'rep'=8,'tp'=8] {'tp'}, use_global_device_ids=true, to_apply=%region_25.26 | all-reduce | flops 128 | bytes 1024 | tf_op jit(solution)/shard_map/psum | solution.py:156
  1242.7 3.3 collective-permute-start.10
  1248.7 39.9 %all_gather.39 = bf16[128,896]{0,1:T(8,128)(2,1)S(1)} all-gather(bf16[128,112]{0,1:T(8,128)(2,1)S(1)} %bitcast_select_fusion.12), channel_id=1, replica_groups=mesh['section'=4,'rep'=8,'tp'=8] {'tp'}, dimensions={1}, use_global_device_ids=true | all-gather | bytes 258048 | tf_op jit(solution)/shard_map/all_gather | solution.py:35
  1292.2 7.5 fusion.21
  1299.7 3.1 copy.51
  1302.9 3.9 fusion.19
  1311.6 12.1 stack_reshape.10
  1323.6 4.9 fusion.20
  1330.1 4.0 reshape.169
  1334.0 11.3 stack_reshape.9
  1345.4 7.8 pad_maximum_fusion
  1353.2 138.0 %conditional.2 = (bf16[3,544768]{1,0:T(4,128)(2,1)}, bf16[1,544768]{1,0:T(2,128)(2,1)}, bf16[1,544768]{1,0:T(2,128)(2,1)}, bf16[1,544768]{1,0:T(2,128)(2,1)}, bf...) conditional(s32[]{:T(128)} %clamp.3, ...), branch_computations={%region_30.31_spmd, %region_31.32_spmd, %region_32.33_spmd} | conditional | flops 8171520 | bytes 56655996
  1354.3 10.7 collective-permute-start.2
  1365.0 81.6 %collective-permute-done.2 = bf16[3,544768]{1,0:T(4,128)(2,1)S(1)} collective-permute-done((bf16[3,544768]{1,0:T(4,128)(2,1)S(1)}, bf16[3,544768]{1,0:T(4,128)(2,1)S(1)}, u32[]{:S(2)}, u32[]{:S(2)}) %collective-permute-start.2) | collective-permute-done | bytes 3268640 | tf_op jit(solution)/shard_map/cond/branch_2_fun/ppermute | solution.py:25
  1446.6 2.9 add_multiply_fusion.2
  1449.5 32.6 %fusion.237 = (bf16[544768]{0:T(1024)(128)(2,1)S(1)}, bf16[1,544768]{1,0:T(2,128)(2,1)}, bf16[544768]{0:T(1024)(128)(2,1)}, bf16[1,544768]{1,0:T(2,128)(2,1)}, b...) fusion(bf16[3,544768]{1,0:T(4,128)(2,1)S(1)} %add_multiply_fusion.2), kind=kLoop, calls=%fused_computation.386 | loop fusion | bytes 9805824 | tf_op jit(solution)/shard_map/slice | solution.py:182
  1492.3 31.5 %psum.39 = f32[128]{0:T(128)S(1)} all-reduce(f32[128]{0:T(128)S(1)} %fusion.189), channel_id=1, replica_groups=mesh['section'=4,'rep'=8,'tp'=8] {'tp'}, use_global_device_ids=true, to_apply=%region_29.30 | all-reduce | flops 128 | bytes 1024 | tf_op jit(solution)/shard_map/psum | solution.py:156
  (257 shorter events, 115.7 us)
Async XLA Ops:
  7.2 128.5 %reduce-scatter.11.cloned.1.call-start = ((), (), s32[]{:S(2)}) async-start(), calls=%async_computation.10 | async-start | bytes 258048 | tf_op jit(solution)/shard_map/reduce_scatter | solution.py:106
  59.2 124.3 %copy-start.3 = (bf16[1,1,896,608]{2,3,1,0:T(8,128)(2,1)S(1)}, bf16[1,1,896,608]{2,3,1,0:T(8,128)(2,1)}, u32[]{:S(2)}) copy-start(bf16[1,1,896,608]{2,3,1,0:T(8,128)(2,1)} %param.18) | copy-start | bytes 3268612
  59.2 204.0 %reduce-scatter.13.cloned.1.call-start = ((), (), s32[]{:S(2)}) async-start(), calls=%async_computation.11 | async-start | bytes 258048 | tf_op jit(solution)/shard_map/reduce_scatter | solution.py:106
  136.5 5.8 collective-permute-start.3
  187.1 203.6 %reduce-scatter.15.cloned.1.call-start = ((), (), s32[]{:S(2)}) async-start(), calls=%async_computation.12 | async-start | bytes 258048 | tf_op jit(solution)/shard_map/reduce_scatter | solution.py:106
  264.0 5.8 collective-permute-start.4
  267.6 47.0 %copy-start.26 = (bf16[1,128,112]{1,0,2:T(2,128)(2,1)}, bf16[1,128,112]{1,0,2:T(2,128)(2,1)S(1)}, u32[]{:S(2)}) copy-start(bf16[1,128,112]{1,0,2:T(2,128)(2,1)S(1)} %get-tuple-element.116) | copy-start | bytes 86020
  269.8 43.5 %copy-start.34 = (bf16[128,112]{0,1:T(8,128)(2,1)}, bf16[128,112]{0,1:T(8,128)(2,1)S(1)}, u32[]{:S(2)}) copy-start(bf16[128,112]{0,1:T(8,128)(2,1)S(1)} %bitcast_select_fusion.18) | copy-start | bytes 86020
  314.6 248.6 %reduce-scatter.17.cloned.1.call-start = ((), (), s32[]{:S(2)}) async-start(), calls=%async_computation.13 | async-start | bytes 258048 | tf_op jit(solution)/shard_map/reduce_scatter | solution.py:106
  391.4 47.2 %collective-permute-start.5 = (bf16[128,112]{0,1:T(8,128)(2,1)S(1)}, bf16[128,112]{0,1:T(8,128)(2,1)S(1)}, u32[]{:S(2)}, u32[]{:S(2)}) collective-permute-start(bf16[128,112]{0,1:T(8,128)(2,1)S(1)} %get-tuple-element.80), channel_id=1, source_target_pairs={{0,64},{64,128},{128,192},{1,65},{65,129},{129,193},{2,66},{66,130... | collective-permute-start | bytes 86024 | tf_op jit(solution)/shard_map/ppermute | solution.py:31
  439.4 44.1 %copy-start.33 = (bf16[128,112]{0,1:T(8,128)(2,1)}, bf16[128,112]{0,1:T(8,128)(2,1)S(1)}, u32[]{:S(2)}) copy-start(bf16[128,112]{0,1:T(8,128)(2,1)S(1)} %bitcast_select_fusion.17) | copy-start | bytes 86020
  487.6 212.0 %reduce-scatter.21.cloned.1.call-start = ((), (), s32[]{:S(2)}) async-start(), calls=%async_computation.15 | async-start | bytes 258048 | tf_op jit(solution)/shard_map/reduce_scatter | solution.py:152
  564.0 50.0 %copy-start.18 = (bf16[2,128,112]{1,2,0:T(8,128)(2,1)}, bf16[2,128,112]{1,2,0:T(8,128)(2,1)S(1)}, u32[]{:S(2)}) copy-start(bf16[2,128,112]{1,2,0:T(8,128)(2,1)S(1)} %get-tuple-element.77) | copy-start | bytes 172036
  564.0 5.8 collective-permute-start.6
  570.6 41.2 %copy-start.28 = (bf16[128,112]{0,1:T(8,128)(2,1)}, bf16[128,112]{0,1:T(8,128)(2,1)S(1)}, u32[]{:S(2)}) copy-start(bf16[128,112]{0,1:T(8,128)(2,1)S(1)} %bitcast_select_fusion.16) | copy-start | bytes 86020
  618.4 10.7 copy-start.43
  618.4 10.7 copy-start.44
  623.3 152.9 %reduce-scatter.19.cloned.1.call-start = ((), (), s32[]{:S(2)}) async-start(), calls=%async_computation.14 | async-start | bytes 258048 | tf_op jit(solution)/shard_map/reduce_scatter | solution.py:106
  629.0 96.1 %copy-start.27 = (bf16[1,128,112]{1,0,2:T(2,128)(2,1)S(1)}, bf16[1,128,112]{1,0,2:T(2,128)(2,1)}, u32[]{:S(2)}) copy-start(bf16[1,128,112]{1,0,2:T(2,128)(2,1)} %copy-done.26) | copy-start | bytes 86020
  629.0 147.2 %copy-start.19 = (bf16[2,128,112]{1,2,0:T(8,128)(2,1)S(1)}, bf16[2,128,112]{1,2,0:T(8,128)(2,1)}, u32[]{:S(2)}) copy-start(bf16[2,128,112]{1,2,0:T(8,128)(2,1)} %copy-done.18) | copy-start | bytes 172036
  629.0 147.2 %copy-start.29 = (bf16[128,112]{0,1:T(8,128)(2,1)S(1)}, bf16[128,112]{0,1:T(8,128)(2,1)}, u32[]{:S(2)}) copy-start(bf16[128,112]{0,1:T(8,128)(2,1)} %copy-done.28) | copy-start | bytes 86020
  629.0 148.7 %copy-start.39 = (bf16[1,128,112]{1,0,2:T(2,128)(2,1)S(1)}, bf16[1,128,112]{1,0,2:T(2,128)(2,1)}, u32[]{:S(2)}) copy-start(bf16[1,128,112]{1,0,2:T(2,128)(2,1)} %get-tuple-element.115) | copy-start | bytes 86020
  629.0 271.1 %reduce-scatter.23.cloned.1.call-start = ((), (), s32[]{:S(2)}) async-start(), calls=%async_computation.16 | async-start | bytes 258048 | tf_op jit(solution)/shard_map/reduce_scatter | solution.py:152
  725.9 51.8 %collective-permute-start.7 = (bf16[128,112]{0,1:T(8,128)(2,1)S(1)}, bf16[128,112]{0,1:T(8,128)(2,1)}, u32[]{:S(2)}, u32[]{:S(2)}) collective-permute-start(bf16[128,112]{0,1:T(8,128)(2,1)S(1)} %get-tuple-element.76), channel_id=1, source_target_pairs={{64,0},{128,64},{192,128},{65,1},{129,65},{193,129},{66,2},{130,66... | collective-permute-start | bytes 86024 | tf_op jit(solution)/shard_map/ppermute | solution.py:31
  824.0 234.1 %reduce-scatter.25.cloned.1.call-start = ((), (), s32[]{:S(2)}) async-start(), calls=%async_computation.17 | async-start | bytes 258048 | tf_op jit(solution)/shard_map/reduce_scatter | solution.py:152
  829.7 103.0 %copy-start.38 = (bf16[1,128,112]{1,0,2:T(2,128)(2,1)S(1)}, bf16[1,128,112]{1,0,2:T(2,128)(2,1)}, u32[]{:S(2)}) copy-start(bf16[1,128,112]{1,0,2:T(2,128)(2,1)} %get-tuple-element.114) | copy-start | bytes 86020
  925.6 47.4 %copy-start.55 = (bf16[1,1,608,896]{3,2,1,0:T(8,128)(2,1)S(1)}, bf16[1,1,608,896]{3,2,1,0:T(8,128)(2,1)}, u32[]{:S(2)}) copy-start(bf16[1,1,608,896]{3,2,1,0:T(8,128)(2,1)} %param.19) | copy-start | bytes 3268612
  926.6 6.1 collective-permute-start.8
  977.0 239.3 %reduce-scatter.27.cloned.1.call-start = ((), (), s32[]{:S(2)}) async-start(), calls=%async_computation.18 | async-start | bytes 258048 | tf_op jit(solution)/shard_map/reduce_scatter | solution.py:152
  982.6 108.0 %copy-start.37 = (bf16[1,128,112]{1,0,2:T(2,128)(2,1)S(1)}, bf16[1,128,112]{1,0,2:T(2,128)(2,1)}, u32[]{:S(2)}) copy-start(bf16[1,128,112]{1,0,2:T(2,128)(2,1)} %get-tuple-element.113) | copy-start | bytes 86020
  1083.6 47.6 %copy-start.56 = (bf16[1,1,608,896]{3,2,1,0:T(8,128)(2,1)S(1)}, bf16[1,1,608,896]{3,2,1,0:T(8,128)(2,1)}, u32[]{:S(2)}) copy-start(bf16[1,1,608,896]{3,2,1,0:T(8,128)(2,1)} %param.19) | copy-start | bytes 3268612
  1084.5 6.0 collective-permute-start.9
  1135.2 356.1 %reduce-scatter.29.cloned.1.call-start = ((), (), s32[]{:S(2)}) async-start(), calls=%async_computation.19 | async-start | bytes 258048 | tf_op jit(solution)/shard_map/reduce_scatter | solution.py:152
  1140.9 107.9 %copy-start.36 = (bf16[1,128,112]{1,0,2:T(2,128)(2,1)S(1)}, bf16[1,128,112]{1,0,2:T(2,128)(2,1)}, u32[]{:S(2)}) copy-start(bf16[1,128,112]{1,0,2:T(2,128)(2,1)} %get-tuple-element.112) | copy-start | bytes 86020
  1241.7 46.9 %copy-start.57 = (bf16[1,1,608,896]{3,2,1,0:T(8,128)(2,1)S(1)}, bf16[1,1,608,896]{3,2,1,0:T(8,128)(2,1)}, u32[]{:S(2)}) copy-start(bf16[1,1,608,896]{3,2,1,0:T(8,128)(2,1)} %param.19) | copy-start | bytes 3268612
  1242.7 6.0 collective-permute-start.10
  1292.1 10.7 copy-start.9
  1292.1 10.7 copy-start.10
  1292.1 10.7 copy-start.11
  1292.2 10.7 copy-start.58
  1292.2 10.7 copy-start.59
  1311.6 12.1 copy-start.7
  1311.6 12.1 copy-start.60
  1330.1 15.3 %copy-start.6 = (bf16[1,544768]{1,0:T(2,128)(2,1)S(1)}, bf16[1,544768]{1,0:T(2,128)(2,1)}, u32[]{:S(2)}) copy-start(bf16[1,544768]{1,0:T(2,128)(2,1)} %stack_reshape.10) | copy-start | bytes 3268612
  1334.0 11.4 copy-start.5
  1354.3 92.3 %collective-permute-start.2 = (bf16[3,544768]{1,0:T(4,128)(2,1)S(1)}, bf16[3,544768]{1,0:T(4,128)(2,1)S(1)}, u32[]{:S(2)}, u32[]{:S(2)}) collective-permute-start(bf16[3,544768]{1,0:T(4,128)(2,1)S(1)} %param.2), channel_id=1, source_target_pairs={{0,32},{8,40},{16,48},{24,56},{32,0},{40,8},{48,16},{56,24},{1,33}... | collective-permute-start | bytes 9805832 | tf_op jit(solution)/shard_map/cond/branch_2_fun/ppermute | solution.py:25
  1449.5 32.6 %copy-start.2 = (bf16[3,544768]{1,0:T(4,128)(2,1)}, bf16[3,544768]{1,0:T(4,128)(2,1)S(1)}, u32[]{:S(2)}) copy-start(bf16[3,544768]{1,0:T(4,128)(2,1)S(1)} %add_multiply_fusion.2) | copy-start | bytes 9805828 | tf_op jit(solution)/shard_map/conditional
  1491.3 34.2 %copy-start.16 = (bf16[1,1,896,608]{2,3,1,0:T(8,128)(2,1)}, bf16[1,1,896,608]{2,3,1,0:T(8,128)(2,1)S(1)}, u32[]{:S(2)}) copy-start(bf16[1,1,896,608]{2,3,1,0:T(8,128)(2,1)S(1)} %get-tuple-element.44) | copy-start | bytes 3268612
  (30 other events, 61.5 us)
Sparse Core Ops, SparseCore 0:
  59.3 76.3 reduce-scatter.10
  187.2 75.9 reduce-scatter.12
  314.7 75.9 reduce-scatter.14
  487.7 75.4 reduce-scatter.16
  623.5 76.0 reduce-scatter.20
  703.1 73.1 reduce-scatter.18
  824.1 76.0 reduce-scatter.22
  977.2 80.9 reduce-scatter.24
  1135.3 80.9 reduce-scatter.26
  1292.2 80.7 reduce-scatter.28
where the time goes:
time: 1540 us; the launch traced here: 1530 us
  waiting for transfers between devices  729 us (47%)
  blocking collectives  544 us (35%)
  local copies, waits for them, and re-layouts  88.1 us (6%)
  matrix products  87.2 us (6%)
  starting transfers between devices  34.7 us (2%)
  other arithmetic  32.1 us (2%)
  between operations  16 us (1%)
    all_gather x10, blocking collectives, widen(): return lax.all_gather(value, 'tp', axis=1, tiled=True)  414 us
    reduce_scatter x5, waiting for transfers between devices, on_device(): lax.psum_scatter(partial_out.astype(jnp.bfloat16), 'tp', scatter_dimensio...  349 us
    reduce_scatter x5, waiting for transfers between devices, on_device(): lax.psum_scatter(partial_in.astype(jnp.bfloat16), 'tp', scatter_dimension...  290 us
    psum x5, blocking collectives, on_device(): stat = lax.psum(jnp.sum(dnorm_local * normed_local, axis=1), 'tp') / D  130 us
    ppermute x1, waiting for transfers between devices, from_behind(): lax.ppermute(array, axis, [(i, (i + by) % peers) for i in range(peers)])  81.6 us
    dot_general x30, matrix products, contract(): lax.dot_general(left, right, (((left_dim,), (right_dim,)), ((), ())), pre...  64.8 us
    slice x1, local copies, waits for them, and re-layouts, on_device(): new_down = averaged[2].reshape(wd.shape)[None, None]  32.6 us
  transfers between devices with their start and end apart: 19, of which 13 were waited for; matrix products, arithmetic and copies ran while one was open for 9% of the time, Pallas kernels for 0%

commit v1 on v0

--- a/solution.py
+++ b/solution.py
@@ -153,7 +153,9 @@
             partial_in.astype(jnp.bfloat16), "tp", scatter_dimension=1, tiled=True
         ).astype(jnp.float32)
         normed_local = lax.dynamic_slice_in_dim(normed, part * local_width, local_width, 1)
-        stat = lax.psum(jnp.sum(dnorm_local * normed_local, axis=1), "tp") / D
+        stat = (
+            jnp.sum(lax.all_gather(jnp.sum(dnorm_local * normed_local, axis=1), "tp"), axis=0) / D
+        )
         dx_local = (
             dy_local.astype(jnp.float32) + (dnorm_local - normed_local * stat[:, None]) / rms
         ).astype(jnp.bfloat16)

time: 1540 us -> 1530 us (level)
    psum x5 -> x0, blocking collectives: 130 us -> none  [on_device(): stat = lax.psum(jnp.sum(dnorm_local * normed_local, axis=1), 'tp') / D]
    all_gather x0 -> x5, blocking collectives: none -> 125 us  [on_device(): lax.all_gather(jnp.sum(dnorm_local * normed_local, axis=1), 'tp')]
where the time goes in v1:
time: 1530 us
  waiting for transfers between devices  729 us (48%)
  blocking collectives  540 us (35%)
  matrix products  87.3 us (6%)
  local copies, waits for them, and re-layouts  85.3 us (6%)
  starting transfers between devices  34.7 us (2%)
  other arithmetic  32.2 us (2%)
  between operations  16 us (1%)
    all_gather x10, blocking collectives, widen(): return lax.all_gather(value, 'tp', axis=1, tiled=True)  415 us
    reduce_scatter x5, waiting for transfers between devices, on_device(): lax.psum_scatter(partial_out.astype(jnp.bfloat16), 'tp', scatter_dimensio...  350 us
    reduce_scatter x5, waiting for transfers between devices, on_device(): lax.psum_scatter(partial_in.astype(jnp.bfloat16), 'tp', scatter_dimension...  290 us
    all_gather x5, blocking collectives, on_device(): lax.all_gather(jnp.sum(dnorm_local * normed_local, axis=1), 'tp')  125 us
    ppermute x1, waiting for transfers between devices, from_behind(): lax.ppermute(array, axis, [(i, (i + by) % peers) for i in range(peers)])  81.4 us
    dot_general x30, matrix products, contract(): lax.dot_general(left, right, (((left_dim,), (right_dim,)), ((), ())), pre...  64.9 us
    slice x1, local copies, waits for them, and re-layouts, on_device(): new_down = averaged[2].reshape(wd.shape)[None, None]  31.7 us
  transfers between devices with their start and end apart: 19, of which 13 were waited for; matrix products, arithmetic and copies ran while one was open for 9% of the time, Pallas kernels for 0%

profile of v1, /device:TPU:66, one launch (start us, length us, event | category | flops | bytes accessed | tf_op | source)
XLA Modules:
  0.0 1526.2 jit_solution(10482373815532284132)
XLA Ops:
  9.0 44.1 %all-gather = bf16[1,128,896]{1,2,0:T(8,128)(2,1)S(1)} all-gather(bf16[1,128,112]{1,2,0:T(8,128)(2,1)S(1)} %copy_select_fusion.1), channel_id=2, replica_groups=mesh['section'=4,'rep'=8,'tp'=8] {'tp'}, dimensions={2}, use_global_device_ids=true | all-gather | bytes 258048 | tf_op jit(solution)/shard_map/all_gather | solution.py:35
  59.2 76.5 %reduce-scatter.11.cloned.1.call-done = bf16[128,112]{0,1:T(8,128)(2,1)} async-done(((bf16[128,896]{0,1:T(8,128)(2,1)}), bf16[128,112]{0,1:T(8,128)(2,1)}) %reduce-scatter.11.cloned.1.call-update) | async-done | bytes 28688 | tf_op jit(solution)/shard_map/reduce_scatter | solution.py:106
  139.1 3.1 collective-permute-done.3
  142.3 40.6 %all_gather.61 = bf16[128,896]{0,1:T(8,128)(2,1)S(1)} all-gather(bf16[128,112]{0,1:T(8,128)(2,1)S(1)} %bitcast_select_fusion.19), channel_id=1, replica_groups=mesh['section'=4,'rep'=8,'tp'=8] {'tp'}, dimensions={1}, use_global_device_ids=true | all-gather | bytes 258048 | tf_op jit(solution)/shard_map/all_gather | solution.py:35
  187.2 76.0 %reduce-scatter.13.cloned.1.call-done = bf16[128,112]{0,1:T(8,128)(2,1)} async-done(((bf16[128,896]{0,1:T(8,128)(2,1)}), bf16[128,112]{0,1:T(8,128)(2,1)}) %reduce-scatter.13.cloned.1.call-update) | async-done | bytes 28688 | tf_op jit(solution)/shard_map/reduce_scatter | solution.py:106
  269.8 40.6 %all_gather.62 = bf16[128,896]{0,1:T(8,128)(2,1)S(1)} all-gather(bf16[128,112]{0,1:T(8,128)(2,1)S(1)} %bitcast_select_fusion.18), channel_id=1, replica_groups=mesh['section'=4,'rep'=8,'tp'=8] {'tp'}, dimensions={1}, use_global_device_ids=true | all-gather | bytes 258048 | tf_op jit(solution)/shard_map/all_gather | solution.py:35
  315.4 75.3 %reduce-scatter.15.cloned.1.call-done = bf16[128,112]{0,1:T(8,128)(2,1)} async-done(((bf16[128,896]{0,1:T(8,128)(2,1)}), bf16[128,112]{0,1:T(8,128)(2,1)}) %reduce-scatter.15.cloned.1.call-update) | async-done | bytes 28688 | tf_op jit(solution)/shard_map/reduce_scatter | solution.py:106
  394.1 43.7 %all-gather.1 = bf16[1,128,896]{1,2,0:T(8,128)(2,1)} all-gather(bf16[1,128,112]{1,2,0:T(8,128)(2,1)} %copy_select_fusion), channel_id=3, replica_groups=mesh['section'=4,'rep'=8,'tp'=8] {'tp'}, dimensions={2}, use_global_device_ids=true | all-gather | bytes 258048 | tf_op jit(solution)/shard_map/all_gather | solution.py:35
  439.3 44.0 %all_gather.63 = bf16[128,896]{0,1:T(8,128)(2,1)S(1)} all-gather(bf16[128,112]{0,1:T(8,128)(2,1)S(1)} %bitcast_select_fusion.17), channel_id=1, replica_groups=mesh['section'=4,'rep'=8,'tp'=8] {'tp'}, dimensions={1}, use_global_device_ids=true | all-gather | bytes 258048 | tf_op jit(solution)/shard_map/all_gather | solution.py:35
  488.7 74.5 %reduce-scatter.17.cloned.1.call-done = bf16[128,112]{0,1:T(8,128)(2,1)} async-done(((bf16[128,896]{0,1:T(8,128)(2,1)}), bf16[128,112]{0,1:T(8,128)(2,1)}) %reduce-scatter.17.cloned.1.call-update) | async-done | bytes 28688 | tf_op jit(solution)/shard_map/reduce_scatter | solution.py:106
  570.6 41.1 %all_gather.64 = bf16[128,896]{0,1:T(8,128)(2,1)S(1)} all-gather(bf16[128,112]{0,1:T(8,128)(2,1)S(1)} %bitcast_select_fusion.16), channel_id=1, replica_groups=mesh['section'=4,'rep'=8,'tp'=8] {'tp'}, dimensions={1}, use_global_device_ids=true | all-gather | bytes 258048 | tf_op jit(solution)/shard_map/all_gather | solution.py:35
  626.2 2.8 fusion.139
  630.6 69.0 %reduce-scatter.21.cloned.1.call-done = bf16[128,112]{0,1:T(8,128)(2,1)} async-done(((bf16[128,896]{0,1:T(8,128)(2,1)}), bf16[128,112]{0,1:T(8,128)(2,1)}) %reduce-scatter.21.cloned.1.call-update) | async-done | bytes 28688 | tf_op jit(solution)/shard_map/reduce_scatter | solution.py:152
  700.4 23.7 %all-gather.7 = f32[8,1,128]{2,1,0:T(1,128)S(1)} all-gather(f32[1,1,128]{2,1,0:T(1,128)S(1)} %bitcast.539), channel_id=4, replica_groups=mesh['section'=4,'rep'=8,'tp'=8] {'tp'}, dimensions={0}, use_global_device_ids=true | all-gather | bytes 4608 | tf_op jit(solution)/shard_map/all_gather | solution.py:157
  725.1 3.3 collective-permute-start.7
  728.3 47.9 %reduce-scatter.19.cloned.1.call-done = bf16[128,112]{0,1:T(8,128)(2,1)} async-done(((bf16[128,896]{0,1:T(8,128)(2,1)}), bf16[128,112]{0,1:T(8,128)(2,1)}) %reduce-scatter.19.cloned.1.call-update) | async-done | bytes 28688 | tf_op jit(solution)/shard_map/reduce_scatter | solution.py:106
  779.1 40.7 %all_gather.68 = bf16[128,896]{0,1:T(8,128)(2,1)S(1)} all-gather(bf16[128,112]{0,1:T(8,128)(2,1)S(1)} %bitcast_select_fusion.15), channel_id=1, replica_groups=mesh['section'=4,'rep'=8,'tp'=8] {'tp'}, dimensions={1}, use_global_device_ids=true | all-gather | bytes 258048 | tf_op jit(solution)/shard_map/all_gather | solution.py:35
  824.1 2.8 fusion.165
  826.9 2.8 fusion.143
  829.7 70.4 %reduce-scatter.23.cloned.1.call-done = bf16[128,112]{0,1:T(8,128)(2,1)} async-done(((bf16[128,896]{0,1:T(8,128)(2,1)}), bf16[128,112]{0,1:T(8,128)(2,1)}) %reduce-scatter.23.cloned.1.call-update) | async-done | bytes 28688 | tf_op jit(solution)/shard_map/reduce_scatter | solution.py:152
  901.0 23.7 %all-gather.8 = f32[8,1,128]{2,1,0:T(1,128)S(1)} all-gather(f32[1,1,128]{2,1,0:T(1,128)S(1)} %bitcast.540), channel_id=5, replica_groups=mesh['section'=4,'rep'=8,'tp'=8] {'tp'}, dimensions={0}, use_global_device_ids=true | all-gather | bytes 4608 | tf_op jit(solution)/shard_map/all_gather | solution.py:157
  925.7 3.3 collective-permute-start.8
  929.0 2.8 fusion.167
  932.4 40.0 %all_gather.71 = bf16[128,896]{0,1:T(8,128)(2,1)S(1)} all-gather(bf16[128,112]{0,1:T(8,128)(2,1)S(1)} %bitcast_select_fusion.14), channel_id=1, replica_groups=mesh['section'=4,'rep'=8,'tp'=8] {'tp'}, dimensions={1}, use_global_device_ids=true | all-gather | bytes 258048 | tf_op jit(solution)/shard_map/all_gather | solution.py:35
  979.2 2.8 fusion.145
  982.0 75.3 %reduce-scatter.25.cloned.1.call-done = bf16[128,112]{0,1:T(8,128)(2,1)} async-done(((bf16[128,896]{0,1:T(8,128)(2,1)}), bf16[128,112]{0,1:T(8,128)(2,1)}) %reduce-scatter.25.cloned.1.call-update) | async-done | bytes 28688 | tf_op jit(solution)/shard_map/reduce_scatter | solution.py:152
  1058.1 23.7 %all-gather.9 = f32[8,1,128]{2,1,0:T(1,128)S(1)} all-gather(f32[1,1,128]{2,1,0:T(1,128)S(1)} %bitcast.541), channel_id=6, replica_groups=mesh['section'=4,'rep'=8,'tp'=8] {'tp'}, dimensions={0}, use_global_device_ids=true | all-gather | bytes 4608 | tf_op jit(solution)/shard_map/all_gather | solution.py:157
  1082.9 3.3 collective-permute-start.9
  1086.2 2.8 fusion.163
  1089.6 39.9 %all_gather.74 = bf16[128,896]{0,1:T(8,128)(2,1)S(1)} all-gather(bf16[128,112]{0,1:T(8,128)(2,1)S(1)} %bitcast_select_fusion.13), channel_id=1, replica_groups=mesh['section'=4,'rep'=8,'tp'=8] {'tp'}, dimensions={1}, use_global_device_ids=true | all-gather | bytes 258048 | tf_op jit(solution)/shard_map/all_gather | solution.py:35
  1136.3 2.9 fusion.147
  1139.2 75.4 %reduce-scatter.27.cloned.1.call-done = bf16[128,112]{0,1:T(8,128)(2,1)} async-done(((bf16[128,896]{0,1:T(8,128)(2,1)}), bf16[128,112]{0,1:T(8,128)(2,1)}) %reduce-scatter.27.cloned.1.call-update) | async-done | bytes 28688 | tf_op jit(solution)/shard_map/reduce_scatter | solution.py:152
  1215.4 23.7 %all-gather.10 = f32[8,1,128]{2,1,0:T(1,128)S(1)} all-gather(f32[1,1,128]{2,1,0:T(1,128)S(1)} %bitcast.542), channel_id=7, replica_groups=mesh['section'=4,'rep'=8,'tp'=8] {'tp'}, dimensions={0}, use_global_device_ids=true | all-gather | bytes 4608 | tf_op jit(solution)/shard_map/all_gather | solution.py:157
  1240.2 3.3 collective-permute-start.10
  1246.2 40.0 %all_gather.77 = bf16[128,896]{0,1:T(8,128)(2,1)S(1)} all-gather(bf16[128,112]{0,1:T(8,128)(2,1)S(1)} %bitcast_select_fusion.12), channel_id=1, replica_groups=mesh['section'=4,'rep'=8,'tp'=8] {'tp'}, dimensions={1}, use_global_device_ids=true | all-gather | bytes 258048 | tf_op jit(solution)/shard_map/all_gather | solution.py:35
  1290.4 7.5 fusion.21
  1298.0 3.1 copy.59
  1301.1 3.9 fusion.19
  1309.8 12.1 stack_reshape.10
  1321.9 5.1 fusion.20
  1330.8 11.3 stack_reshape.9
  1342.2 7.8 pad_maximum_fusion
  1350.0 135.9 %conditional.2 = (bf16[3,544768]{1,0:T(4,128)(2,1)}, bf16[1,544768]{1,0:T(2,128)(2,1)}, bf16[1,544768]{1,0:T(2,128)(2,1)}, bf16[1,544768]{1,0:T(2,128)(2,1)}, bf...) conditional(s32[]{:T(128)} %clamp.3, ...), branch_computations={%region_30.31_spmd, %region_31.32_spmd, %region_32.33_spmd} | conditional | flops 8171520 | bytes 56655996
  1351.1 10.7 collective-permute-start.2
  1361.8 81.4 %collective-permute-done.2 = bf16[3,544768]{1,0:T(4,128)(2,1)S(1)} collective-permute-done((bf16[3,544768]{1,0:T(4,128)(2,1)S(1)}, bf16[3,544768]{1,0:T(4,128)(2,1)S(1)}, u32[]{:S(2)}, u32[]{:S(2)}) %collective-permute-start.2) | collective-permute-done | bytes 3268640 | tf_op jit(solution)/shard_map/cond/branch_2_fun/ppermute | solution.py:25
  1443.1 2.9 add_multiply_fusion.2
  1446.1 31.7 %fusion.237 = (bf16[544768]{0:T(1024)(128)(2,1)S(1)}, bf16[1,544768]{1,0:T(2,128)(2,1)}, bf16[544768]{0:T(1024)(128)(2,1)S(1)}, bf16[1,544768]{1,0:T(2,128)(2,1)...) fusion(bf16[3,544768]{1,0:T(4,128)(2,1)S(1)} %add_multiply_fusion.2), kind=kLoop, calls=%fused_computation.386 | loop fusion | bytes 9805824 | tf_op jit(solution)/shard_map/slice | solution.py:184
  1487.0 30.5 %all-gather.11 = f32[8,1,128]{2,1,0:T(1,128)S(1)} all-gather(f32[1,1,128]{2,1,0:T(1,128)S(1)} %bitcast.543), channel_id=8, replica_groups=mesh['section'=4,'rep'=8,'tp'=8] {'tp'}, dimensions={0}, use_global_device_ids=true | all-gather | bytes 4608 | tf_op jit(solution)/shard_map/all_gather | solution.py:157
  (264 shorter events, 115.1 us)
Async XLA Ops:
  7.2 128.5 %reduce-scatter.11.cloned.1.call-start = ((), (), s32[]{:S(2)}) async-start(), calls=%async_computation.10 | async-start | bytes 258048 | tf_op jit(solution)/shard_map/reduce_scatter | solution.py:106
  59.2 124.3 %copy-start.3 = (bf16[1,1,896,608]{2,3,1,0:T(8,128)(2,1)S(1)}, bf16[1,1,896,608]{2,3,1,0:T(8,128)(2,1)}, u32[]{:S(2)}) copy-start(bf16[1,1,896,608]{2,3,1,0:T(8,128)(2,1)} %param.18) | copy-start | bytes 3268612
  59.2 204.0 %reduce-scatter.13.cloned.1.call-start = ((), (), s32[]{:S(2)}) async-start(), calls=%async_computation.11 | async-start | bytes 258048 | tf_op jit(solution)/shard_map/reduce_scatter | solution.py:106
  136.5 5.8 collective-permute-start.3
  187.1 203.6 %reduce-scatter.15.cloned.1.call-start = ((), (), s32[]{:S(2)}) async-start(), calls=%async_computation.12 | async-start | bytes 258048 | tf_op jit(solution)/shard_map/reduce_scatter | solution.py:106
  264.0 5.8 collective-permute-start.4
  267.6 47.0 %copy-start.26 = (bf16[1,128,112]{1,0,2:T(2,128)(2,1)}, bf16[1,128,112]{1,0,2:T(2,128)(2,1)S(1)}, u32[]{:S(2)}) copy-start(bf16[1,128,112]{1,0,2:T(2,128)(2,1)S(1)} %get-tuple-element.121) | copy-start | bytes 86020
  269.8 43.5 %copy-start.34 = (bf16[128,112]{0,1:T(8,128)(2,1)}, bf16[128,112]{0,1:T(8,128)(2,1)S(1)}, u32[]{:S(2)}) copy-start(bf16[128,112]{0,1:T(8,128)(2,1)S(1)} %bitcast_select_fusion.18) | copy-start | bytes 86020
  314.5 248.7 %reduce-scatter.17.cloned.1.call-start = ((), (), s32[]{:S(2)}) async-start(), calls=%async_computation.13 | async-start | bytes 258048 | tf_op jit(solution)/shard_map/reduce_scatter | solution.py:106
  391.5 47.0 %collective-permute-start.5 = (bf16[128,112]{0,1:T(8,128)(2,1)S(1)}, bf16[128,112]{0,1:T(8,128)(2,1)S(1)}, u32[]{:S(2)}, u32[]{:S(2)}) collective-permute-start(bf16[128,112]{0,1:T(8,128)(2,1)S(1)} %get-tuple-element.85), channel_id=1, source_target_pairs={{0,64},{64,128},{128,192},{1,65},{65,129},{129,193},{2,66},{66,130... | collective-permute-start | bytes 86024 | tf_op jit(solution)/shard_map/ppermute | solution.py:31
  439.3 44.6 %copy-start.33 = (bf16[128,112]{0,1:T(8,128)(2,1)}, bf16[128,112]{0,1:T(8,128)(2,1)S(1)}, u32[]{:S(2)}) copy-start(bf16[128,112]{0,1:T(8,128)(2,1)S(1)} %bitcast_select_fusion.17) | copy-start | bytes 86020
  487.5 212.0 %reduce-scatter.21.cloned.1.call-start = ((), (), s32[]{:S(2)}) async-start(), calls=%async_computation.15 | async-start | bytes 258048 | tf_op jit(solution)/shard_map/reduce_scatter | solution.py:152
  564.0 50.0 %copy-start.18 = (bf16[2,128,112]{1,2,0:T(8,128)(2,1)}, bf16[2,128,112]{1,2,0:T(8,128)(2,1)S(1)}, u32[]{:S(2)}) copy-start(bf16[2,128,112]{1,2,0:T(8,128)(2,1)S(1)} %get-tuple-element.82) | copy-start | bytes 172036
  564.0 5.8 collective-permute-start.6
  570.6 42.2 %copy-start.28 = (bf16[128,112]{0,1:T(8,128)(2,1)}, bf16[128,112]{0,1:T(8,128)(2,1)S(1)}, u32[]{:S(2)}) copy-start(bf16[128,112]{0,1:T(8,128)(2,1)S(1)} %bitcast_select_fusion.16) | copy-start | bytes 86020
  618.4 10.7 copy-start.45
  618.5 10.7 copy-start.46
  623.4 152.8 %reduce-scatter.19.cloned.1.call-start = ((), (), s32[]{:S(2)}) async-start(), calls=%async_computation.14 | async-start | bytes 258048 | tf_op jit(solution)/shard_map/reduce_scatter | solution.py:106
  629.1 95.1 %copy-start.27 = (bf16[1,128,112]{1,0,2:T(2,128)(2,1)S(1)}, bf16[1,128,112]{1,0,2:T(2,128)(2,1)}, u32[]{:S(2)}) copy-start(bf16[1,128,112]{1,0,2:T(2,128)(2,1)} %copy-done.26) | copy-start | bytes 86020
  629.1 147.2 %copy-start.19 = (bf16[2,128,112]{1,2,0:T(8,128)(2,1)S(1)}, bf16[2,128,112]{1,2,0:T(8,128)(2,1)}, u32[]{:S(2)}) copy-start(bf16[2,128,112]{1,2,0:T(8,128)(2,1)} %copy-done.18) | copy-start | bytes 172036
  629.1 147.2 %copy-start.29 = (bf16[128,112]{0,1:T(8,128)(2,1)S(1)}, bf16[128,112]{0,1:T(8,128)(2,1)}, u32[]{:S(2)}) copy-start(bf16[128,112]{0,1:T(8,128)(2,1)} %copy-done.28) | copy-start | bytes 86020
  629.1 148.6 %copy-start.39 = (bf16[1,128,112]{1,0,2:T(2,128)(2,1)S(1)}, bf16[1,128,112]{1,0,2:T(2,128)(2,1)}, u32[]{:S(2)}) copy-start(bf16[1,128,112]{1,0,2:T(2,128)(2,1)} %get-tuple-element.120) | copy-start | bytes 86020
  629.1 271.0 %reduce-scatter.23.cloned.1.call-start = ((), (), s32[]{:S(2)}) async-start(), calls=%async_computation.16 | async-start | bytes 258048 | tf_op jit(solution)/shard_map/reduce_scatter | solution.py:152
  725.1 52.7 %collective-permute-start.7 = (bf16[128,112]{0,1:T(8,128)(2,1)S(1)}, bf16[128,112]{0,1:T(8,128)(2,1)}, u32[]{:S(2)}, u32[]{:S(2)}) collective-permute-start(bf16[128,112]{0,1:T(8,128)(2,1)S(1)} %get-tuple-element.81), channel_id=1, source_target_pairs={{64,0},{128,64},{192,128},{65,1},{129,65},{193,129},{66,2},{130,66... | collective-permute-start | bytes 86024 | tf_op jit(solution)/shard_map/ppermute | solution.py:31
  824.1 233.2 %reduce-scatter.25.cloned.1.call-start = ((), (), s32[]{:S(2)}) async-start(), calls=%async_computation.17 | async-start | bytes 258048 | tf_op jit(solution)/shard_map/reduce_scatter | solution.py:152
  829.7 102.1 %copy-start.38 = (bf16[1,128,112]{1,0,2:T(2,128)(2,1)S(1)}, bf16[1,128,112]{1,0,2:T(2,128)(2,1)}, u32[]{:S(2)}) copy-start(bf16[1,128,112]{1,0,2:T(2,128)(2,1)} %get-tuple-element.119) | copy-start | bytes 86020
  924.7 47.7 %copy-start.57 = (bf16[1,1,608,896]{3,2,1,0:T(8,128)(2,1)S(1)}, bf16[1,1,608,896]{3,2,1,0:T(8,128)(2,1)}, u32[]{:S(2)}) copy-start(bf16[1,1,608,896]{3,2,1,0:T(8,128)(2,1)} %param.19) | copy-start | bytes 3268612
  925.7 6.1 collective-permute-start.8
  976.4 238.1 %reduce-scatter.27.cloned.1.call-start = ((), (), s32[]{:S(2)}) async-start(), calls=%async_computation.18 | async-start | bytes 258048 | tf_op jit(solution)/shard_map/reduce_scatter | solution.py:152
  982.0 107.0 %copy-start.37 = (bf16[1,128,112]{1,0,2:T(2,128)(2,1)S(1)}, bf16[1,128,112]{1,0,2:T(2,128)(2,1)}, u32[]{:S(2)}) copy-start(bf16[1,128,112]{1,0,2:T(2,128)(2,1)} %get-tuple-element.118) | copy-start | bytes 86020
  1081.9 47.7 %copy-start.58 = (bf16[1,1,608,896]{3,2,1,0:T(8,128)(2,1)S(1)}, bf16[1,1,608,896]{3,2,1,0:T(8,128)(2,1)}, u32[]{:S(2)}) copy-start(bf16[1,1,608,896]{3,2,1,0:T(8,128)(2,1)} %param.19) | copy-start | bytes 3268612
  1082.9 6.2 collective-permute-start.9
  1133.6 352.5 %reduce-scatter.29.cloned.1.call-start = ((), (), s32[]{:S(2)}) async-start(), calls=%async_computation.19 | async-start | bytes 258048 | tf_op jit(solution)/shard_map/reduce_scatter | solution.py:152
  1139.2 107.0 %copy-start.36 = (bf16[1,128,112]{1,0,2:T(2,128)(2,1)S(1)}, bf16[1,128,112]{1,0,2:T(2,128)(2,1)}, u32[]{:S(2)}) copy-start(bf16[1,128,112]{1,0,2:T(2,128)(2,1)} %get-tuple-element.117) | copy-start | bytes 86020
  1239.2 47.1 %copy-start.59 = (bf16[1,1,608,896]{3,2,1,0:T(8,128)(2,1)S(1)}, bf16[1,1,608,896]{3,2,1,0:T(8,128)(2,1)}, u32[]{:S(2)}) copy-start(bf16[1,1,608,896]{3,2,1,0:T(8,128)(2,1)} %param.19) | copy-start | bytes 3268612
  1240.2 6.0 collective-permute-start.10
  1290.4 10.7 copy-start.9
  1290.4 10.7 copy-start.10
  1290.4 10.7 copy-start.11
  1290.4 10.7 copy-start.60
  1290.4 10.7 copy-start.61
  1309.8 12.1 copy-start.7
  1309.8 12.1 copy-start.41
  1328.1 14.1 copy-start.6
  1330.8 11.4 copy-start.5
  1351.1 92.0 %collective-permute-start.2 = (bf16[3,544768]{1,0:T(4,128)(2,1)S(1)}, bf16[3,544768]{1,0:T(4,128)(2,1)S(1)}, u32[]{:S(2)}, u32[]{:S(2)}) collective-permute-start(bf16[3,544768]{1,0:T(4,128)(2,1)S(1)} %param.2), channel_id=1, source_target_pairs={{0,32},{8,40},{16,48},{24,56},{32,0},{40,8},{48,16},{56,24},{1,33}... | collective-permute-start | bytes 9805832 | tf_op jit(solution)/shard_map/cond/branch_2_fun/ppermute | solution.py:25
  1446.1 31.7 %copy-start.2 = (bf16[3,544768]{1,0:T(4,128)(2,1)}, bf16[3,544768]{1,0:T(4,128)(2,1)S(1)}, u32[]{:S(2)}) copy-start(bf16[3,544768]{1,0:T(4,128)(2,1)S(1)} %add_multiply_fusion.2) | copy-start | bytes 9805828 | tf_op jit(solution)/shard_map/conditional
  1486.0 33.1 %copy-start.16 = (bf16[1,1,896,608]{2,3,1,0:T(8,128)(2,1)}, bf16[1,1,896,608]{2,3,1,0:T(8,128)(2,1)S(1)}, u32[]{:S(2)}) copy-start(bf16[1,1,896,608]{2,3,1,0:T(8,128)(2,1)S(1)} %get-tuple-element.49) | copy-start | bytes 3268612
  (31 other events, 62.7 us)
Sparse Core Ops, SparseCore 0:
  59.3 76.3 reduce-scatter.10
  187.2 75.9 reduce-scatter.12
  314.7 75.9 reduce-scatter.14
  487.7 75.4 reduce-scatter.16
  623.5 75.9 reduce-scatter.20
  703.1 73.0 reduce-scatter.18
  824.2 75.8 reduce-scatter.22
  976.5 80.6 reduce-scatter.24
  1133.7 80.8 reduce-scatter.26
  1290.5 80.6 reduce-scatter.28
